TPU v7x, 32 devices: a whole 2x2x4 slice. The times are simulated.
32 devices in a mesh: slab: 4 (over y, core), inner: 8 (over z, x).
Axes of the slice: x: 2, y: 2, z: 4, core: 2. Of those that a mesh axis runs over, the one named last changes fastest.
Arguments:
- x_in: bfloat16 [8192, 16384], P(('slab', 'inner')), may hold values from -6 to 6
- bc_in: bfloat16 [8192, 4096], P(('slab', 'inner')), may hold values from -6 to 6
- dt_raw: bfloat16 [8192, 256], P(('slab', 'inner')), may hold values from -6.7 to -4.3
- dt_bias: float32 [256], replicated, may hold values from -0.5 to 0.5
- a_log: float32 [256], replicated, may hold values from -8 to 0, as said below
- d_skip: float32 [256], replicated, may hold values from 0.5 to 1.5
- conv_x_weight: float32 [4, 16384], replicated, may hold values from -3 to 3
- conv_x_bias: float32 [16384], replicated, may hold values from -3 to 3
- conv_bc_weight: float32 [4, 4096], replicated, may hold values from -3 to 3
- conv_bc_bias: float32 [4096], replicated, may hold values from -3 to 3
Outputs:
- y_out: bfloat16 [8192, 16384], P('slab', 'inner')
Inputs may be any that keep to these rules, and one draw needn't show every extreme that they name: `a_log`: per-head logarithm of the decay rate.
All inputs are finite; a program needn't handle non-finite values.
Results may differ from a plain program's by a relative error of at most 0.0034.
Values may be sent and summed in bfloat16 or wider, within the bound.
No kernel may reach another device: no remote copies, remote signals or barrier semaphores. Data moves between devices by JAX's collectives and lax.ppermute only.
A program may use at most 256 MiB of HBM per device.

v0:
```python
import jax
import jax.numpy as jnp
import numpy as np
from jax import lax
from jax.sharding import PartitionSpec as P

HEADS = 256
HEADDIM = 64
STATE = 256
GROUPS = 8
CONV = 4
SPAN = 256


def from_behind(x, axis, by):
    size = lax.axis_size(axis)
    pairs = [(i, i + by) for i in range(size) if 0 <= i + by < size]
    return lax.ppermute(x, axis, pairs)


def causal_conv(row_block, before, weight, conv_bias):
    kernel_len = weight.shape[0]
    length = row_block.shape[0]
    padded = jnp.concatenate([before, row_block], axis=0).astype(jnp.float32)
    summed = conv_bias[None, :] + weight[0][None, :] * padded[0:length]
    for offset in range(1, kernel_len):
        summed = summed + weight[offset][None, :] * padded[offset : offset + length]
    return jax.nn.silu(summed).astype(jnp.bfloat16)


def head_columns(per_head, head_count):
    rows = per_head.shape[0]
    return jnp.broadcast_to(per_head[:, :, None], (rows, head_count, HEADDIM)).reshape(
        rows, head_count * HEADDIM
    )


def span_step(state, pieces):
    x_span, b_span, c_span, dt_span, da_span = pieces
    size_q = x_span.shape[0]
    head_count = dt_span.shape[1]
    cumul = jnp.cumsum(da_span, axis=0).T
    row_ids = lax.broadcasted_iota(jnp.int32, (size_q, size_q), 0)
    col_ids = lax.broadcasted_iota(jnp.int32, (size_q, size_q), 1)
    gaps = cumul[:, :, None] - cumul[:, None, :]
    decays = jnp.where((row_ids >= col_ids)[None], jnp.exp(jnp.minimum(gaps, 0.0)), 0.0)
    scores = jnp.dot(c_span, b_span.T, preferred_element_type=jnp.float32)
    mixing = (decays * scores[None] * dt_span.T[:, None, :]).astype(jnp.bfloat16)
    x_heads = x_span.reshape(size_q, head_count, HEADDIM)
    y_intra = jnp.einsum(
        "hts,shp->thp", mixing, x_heads, preferred_element_type=jnp.float32
    ).reshape(size_q, head_count * HEADDIM)
    y_inter = jnp.dot(c_span, state.astype(jnp.bfloat16), preferred_element_type=jnp.float32)
    y_inter = y_inter * head_columns(jnp.exp(cumul.T), head_count)
    weights_end = (jnp.exp(cumul[:, -1:] - cumul) * dt_span.T).T
    scaled = (x_span.astype(jnp.float32) * head_columns(weights_end, head_count)).astype(
        jnp.bfloat16
    )
    contrib = jnp.dot(b_span.T, scaled, preferred_element_type=jnp.float32)
    end_decay = head_columns(jnp.exp(cumul[:, -1])[None, :], head_count)
    new_state = end_decay * state + contrib
    return (new_state, y_intra + y_inter)


def slab_core(x_rows, b_rows, c_rows, dt_rows, da_rows):
    length = x_rows.shape[0]
    width = x_rows.shape[1]
    head_count = dt_rows.shape[1]
    span_count = length // SPAN
    inputs = (
        x_rows.reshape(span_count, SPAN, width),
        b_rows.reshape(span_count, SPAN, STATE),
        c_rows.reshape(span_count, SPAN, STATE),
        dt_rows.reshape(span_count, SPAN, head_count),
        da_rows.reshape(span_count, SPAN, head_count),
    )
    zero_state = jnp.zeros((STATE, width), jnp.float32)
    end_state, outputs = lax.scan(span_step, zero_state, inputs)
    return (outputs.reshape(length, width), end_state)


def group_copies(bc_rows, dest_group, n_inner):
    tok_rows = bc_rows.shape[0]
    split = bc_rows.reshape(tok_rows, 2, GROUPS, STATE)
    picked = jnp.take(split, dest_group, axis=2)
    return jnp.transpose(picked, (0, 2, 1, 3)).reshape(tok_rows, n_inner, 2 * STATE)


def shards(
    x_in,
    bc_in,
    dt_raw,
    dt_bias,
    a_log,
    d_skip,
    conv_x_weight,
    conv_x_bias,
    conv_bc_weight,
    conv_bc_bias,
):
    n_inner = lax.axis_size("inner")
    n_slab = lax.axis_size("slab")
    tok_dev = x_in.shape[0]
    heads_dev = HEADS // n_inner
    ch_dev = heads_dev * HEADDIM
    per_group = HEADS // GROUPS
    inner_idx = lax.axis_index("inner")
    dest_group = np.arange(n_inner) * heads_dev // per_group
    edge = CONV - 1
    dt_send = dt_raw.reshape(tok_dev, n_inner, heads_dev)
    x_prev, bc_prev = from_behind(
        (x_in[tok_dev - edge :], bc_in[tok_dev - edge :]), ("slab", "inner"), 1
    )
    x_ready = causal_conv(x_in, x_prev, conv_x_weight, conv_x_bias)
    bc_ready = causal_conv(bc_in, bc_prev, conv_bc_weight, conv_bc_bias)
    bc_send = group_copies(bc_ready, dest_group, n_inner)
    x_recv, bc_recv, dt_recv = (
        lax.all_to_all(
            x_ready.reshape(tok_dev, n_inner, ch_dev),
            "inner",
            split_axis=1,
            concat_axis=0,
            tiled=True,
        ),
        lax.all_to_all(bc_send, "inner", split_axis=1, concat_axis=0, tiled=True),
        lax.all_to_all(dt_send, "inner", split_axis=1, concat_axis=0, tiled=True),
    )
    x_slab = x_recv.reshape(-1, ch_dev)
    bc_slab = bc_recv.reshape(-1, 2 * STATE)
    bias_heads = lax.dynamic_slice_in_dim(dt_bias, inner_idx * heads_dev, heads_dev, 0)
    rate_heads = -jnp.exp(lax.dynamic_slice_in_dim(a_log, inner_idx * heads_dev, heads_dev, 0))
    skip_heads = lax.dynamic_slice_in_dim(d_skip, inner_idx * heads_dev, heads_dev, 0)
    dt_heads = jax.nn.softplus(
        dt_recv.reshape(-1, heads_dev).astype(jnp.float32) + bias_heads[None, :]
    )
    da_heads = dt_heads * rate_heads[None, :]
    c_slab = bc_slab[:, STATE:]
    y_local, end_state = slab_core(x_slab, bc_slab[:, :STATE], c_slab, dt_heads, da_heads)
    cum_slab = jnp.cumsum(da_heads, axis=0)
    slab_decay = head_columns(jnp.exp(cum_slab[-1:]), heads_dev)[0]
    incoming = jnp.zeros_like(end_state)
    outgoing = end_state
    for hop_number in range(n_slab - 1):
        incoming = from_behind(outgoing, "slab", 1)
        outgoing = slab_decay[None, :] * incoming + end_state
    carried = jnp.dot(c_slab, incoming.astype(jnp.bfloat16), preferred_element_type=jnp.float32)
    carried = carried * head_columns(jnp.exp(cum_slab), heads_dev)
    skip_cols = jnp.repeat(skip_heads, HEADDIM)
    y_slab = y_local + carried + skip_cols[None, :] * x_slab.astype(jnp.float32)
    return y_slab.astype(jnp.bfloat16)


def solution(mesh):
    placed = (
        P(("slab", "inner"), None),
        P(("slab", "inner"), None),
        P(("slab", "inner"), None),
        P(),
        P(),
        P(),
        P(),
        P(),
        P(),
        P(),
    )
    return jax.shard_map(
        shards, mesh=mesh, in_specs=placed, out_specs=P("slab", "inner"), check_vma=False
    )
```

profile of v0, /device:TPU:0, one launch (start us, length us, event | category | flops | bytes accessed | tf_op | source)
XLA Modules:
  0.0 606.8 jit_solution(15291614099124217635)
XLA Ops:
  1.7 7.3 %all-to-all-start = ((bf16[256,8,32]{0,2,1:T(8,128)(2,1)}), bf16[256,8,32]{0,2,1:T(8,128)(2,1)S(1)}, u32[]{:S(2)}, u32[]{:S(2)}) async-start(bf16[256,8,32]{0,2,1:T(8,128)(2,1)} %bitcast), calls=%async_computation | async-start | bytes 262144 | tf_op jit(solution)/shard_map/all_to_all | solution.py:126
  9.8 4.5 collective-permute-start
  29.7 7.0 %multiply_convert_fusion.4 = bf16[256,4096]{0,1:T(8,128)(2,1)S(1)} fusion(f32[259,4096]{0,1:T(8,128)S(1)} %maximum_convert_fusion.1, f32[4096]{0:T(1024)S(1)} %bitcast.210, f32[4096]{0:T(1024)S(1)} %bitcast.211, f32[4096]{0:T(1024)S(1)} %bitcast.209, f32[4096]{0:T(1024)S(1)} %bitcast.208, f32[4096]{0:T(1024)S(1)} %copy-done.6), kind=kLoop, calls=%fused_computation.66 | loop fusion | flops 13631488 | bytes 18956288 | tf_op jit(solution)/shard_map/convert_element_type | solution.py:28
  47.0 11.8 %maximum_convert_fusion = f32[259,16384]{1,0:T(8,128)} fusion(bf16[256,16384]{1,0:T(8,128)(2,1)} %param.13, bf16[3,16384]{1,0:T(4,128)(2,1)} %collective-permute-done.1), kind=kLoop, calls=%fused_computation.56 | loop fusion | flops 16973824 | bytes 25460736 | tf_op jit(solution)/shard_map/convert_element_type | solution.py:24
  58.8 4.0 all-to-all-start.1
  62.8 27.1 %multiply_convert_fusion.3 = bf16[256,16384]{1,0:T(8,128)(2,1)} fusion(f32[259,16384]{1,0:T(8,128)} %maximum_convert_fusion, f32[16384]{0:T(1024)S(1)} %bitcast.204, f32[16384]{0:T(1024)S(1)} %bitcast.205, f32[16384]{0:T(1024)S(1)} %bitcast.203, f32[16384]{0:T(1024)S(1)} %bitcast.202, f32[16384]{0:T(1024)S(1)} %copy-done.5), kind=kLoop, calls=%fused_computation.55 | loop fusion | flops 54525952 | bytes 75825152 | tf_op jit(solution)/shard_map/convert_element_type | solution.py:28
  89.9 11.9 %copy.96 = bf16[256,16384]{0,1:T(8,128)(2,1)} copy(bf16[256,16384]{1,0:T(8,128)(2,1)} %multiply_convert_fusion.3) | data formatting | bytes 16777216 | tf_op jit(solution)/shard_map/convert_element_type | solution.py:28
  101.9 10.6 %all-to-all-done.1 = bf16[256,8,512]{0,2,1:T(8,128)(2,1)S(1)} async-done(((bf16[256,8,512]{0,2,1:T(8,128)(2,1)}), bf16[256,8,512]{0,2,1:T(8,128)(2,1)S(1)}, u32[]{:S(2)}, u32[]{:S(2)}) %all-to-all-start.1) | async-done | bytes 2097184 | tf_op jit(solution)/shard_map/all_to_all | solution.py:125
  113.7 5.1 all-to-all-start.2
  127.1 175.1 %all-to-all-done.2 = bf16[256,8,2048]{0,2,1:T(8,128)(2,1)} async-done(((bf16[256,8,2048]{0,2,1:T(8,128)(2,1)}), bf16[256,8,2048]{0,2,1:T(8,128)(2,1)}, u32[]{:S(2)}, u32[]{:S(2)}) %all-to-all-start.2) | async-done | bytes 8388640 | tf_op jit(solution)/shard_map/all_to_all | solution.py:118
  302.1 194.8 %while.13 = (s32[]{:T(128)}, f32[256,2048]{1,0:T(8,128)S(1)}, f32[8,256,2048]{2,1,0:T(8,128)}, f32[8,256,32]{1,2,0:T(8,128)}, bf16[8,256,256]{2,1,0:T(8,128)(2,1...) while((s32[]{:T(128)}, f32[256,2048]{1,0:T(8,128)S(1)}, ...), condition=%wide.region_3.4_spmd.clone, body=%wide.region_0.3_spmd.clone.sunk | while | flops 857301120 | bytes 33167368 | solution.py:78
  307.3 4.2 fusion.72
  318.8 4.1 fusion.73
  331.7 4.2 fusion.72
  356.0 4.2 fusion.72
  367.5 4.0 fusion.73
  380.4 4.2 fusion.72
  391.9 4.1 fusion.73
  404.7 4.2 fusion.72
  416.2 4.1 fusion.73
  429.1 4.2 fusion.72
  440.6 4.0 fusion.73
  453.4 4.2 fusion.72
  465.0 4.0 fusion.73
  477.8 4.2 fusion.72
  499.9 9.1 %reduce-window.16 = f32[32,16,128]{2,1,0:T(8,128)S(1)} reduce-window(f32[32,16,128]{2,1,0:T(8,128)S(1)} %bitcast.199, f32[]{:T(128)} %constant.44.clone.1), window={size=1x1x128 pad=0_0x0_0x127_0}, to_apply=%region_4.5 | reduce-window | flops 8323072 | bytes 524292 | tf_op jit(solution)/shard_map/reduce-window.2
  513.4 14.0 %collective-permute-start.3 = (f32[256,2048]{1,0:T(8,128)}, f32[256,2048]{1,0:T(8,128)}, u32[]{:S(2)}, u32[]{:S(2)}) collective-permute-start(f32[256,2048]{1,0:T(8,128)} %multiply_add_fusion.1), channel_id=1, source_target_pairs={{0,8},{8,16},{16,24},{1,9},{9,17},{17,25},{2,10},{10,18},{18,26},{... | collective-permute-start | bytes 6291464 | tf_op jit(solution)/shard_map/ppermute | solution.py:18
  527.7 7.8 %broadcast_in_dim.88 = f32[2048,32,64]{0,2,1:T(8,128)} broadcast(f32[2048,32]{0,1:T(8,128)S(1)} %fusion.47), dimensions={0,1} | broadcast | bytes 17039360 | tf_op jit(solution)/shard_map/broadcast_in_dim | solution.py:33
  535.6 17.6 %copy.100 = f32[2048,2048]{1,0:T(8,128)} copy(f32[2048,2048]{0,1:T(8,128)} %bitcast.189) | data formatting | bytes 33554432 | tf_op jit(solution)/shard_map/reshape | solution.py:33
  559.3 10.6 %bitcast_convert_fusion = f32[8,256,1,2048]{1,3,0,2:T(8,128)} fusion(bf16[256,8,2048]{0,2,1:T(8,128)(2,1)} %all-to-all-done.2), kind=kLoop, calls=%fused_computation.57 | loop fusion | flops 4194304 | bytes 25165824 | tf_op jit(solution)/shard_map/convert_element_type | solution.py:149
  569.9 16.6 %copy.101 = f32[8,256,1,2048]{3,1,0,2:T(8,128)} copy(f32[8,256,1,2048]{1,3,0,2:T(8,128)} %bitcast_convert_fusion) | data formatting | bytes 33554432 | tf_op jit(solution)/shard_map/convert_element_type | solution.py:149
  586.5 20.3 %fusion.31 = bf16[2048,2048]{1,0:T(8,128)(2,1)} fusion(f32[8,256,1,2048]{3,1,0,2:T(8,128)} %copy.101, f32[8,256,2048]{2,1,0:T(8,128)} %get-tuple-element.48, f32[2048,2048]{1,0:T(8,128)} %copy.100, f32[2048]{0:T(1024)S(1)} %mul.208, bf16[256,2048]{1,0:T(8,128)(2,1)S(1)} %collective-permute-done.4, bf16[2048,512]{1,0:T(8,128)(2,1)S(1)} %bitcast.193), kind=kOutput, calls=%fused_computation.53 | convolution fusion | flops 2168455168 | bytes 60825600 | tf_op jit(solution)/shard_map/dot_general | solution.py:146
  (225 shorter events, 187.8 us)
Async XLA Ops:
  1.7 57.1 %all-to-all-start = ((bf16[256,8,32]{0,2,1:T(8,128)(2,1)}), bf16[256,8,32]{0,2,1:T(8,128)(2,1)S(1)}, u32[]{:S(2)}, u32[]{:S(2)}) async-start(bf16[256,8,32]{0,2,1:T(8,128)(2,1)} %bitcast), calls=%async_computation | async-start | bytes 262144 | tf_op jit(solution)/shard_map/all_to_all | solution.py:126
  9.8 17.2 %collective-permute-start = (bf16[3,4096]{1,0:T(4,128)(2,1)S(1)}, bf16[3,4096]{1,0:T(4,128)(2,1)}, u32[]{:S(2)}, u32[]{:S(2)}) collective-permute-start(bf16[3,4096]{1,0:T(4,128)(2,1)S(1)} %slice.80), channel_id=1, source_target_pairs={{0,1},{1,2},{2,3},{3,4},{4,5},{5,6},{6,7},{7,8},{8,9},{9,10},{10,1... | collective-permute-start | bytes 73736 | tf_op jit(solution)/shard_map/ppermute | solution.py:18
  16.0 31.0 %collective-permute-start.1 = (bf16[3,16384]{1,0:T(4,128)(2,1)}, bf16[3,16384]{1,0:T(4,128)(2,1)}, u32[]{:S(2)}, u32[]{:S(2)}) collective-permute-start(bf16[3,16384]{1,0:T(4,128)(2,1)} %slice.90), channel_id=1, source_target_pairs={{0,1},{1,2},{2,3},{3,4},{4,5},{5,6},{6,7},{7,8},{8,9},{9,10},{10,1... | collective-permute-start | bytes 294920 | tf_op jit(solution)/shard_map/ppermute | solution.py:18
  28.3 1.4 copy-start.2
  28.3 1.4 copy-start.3
  28.3 1.4 copy-start.4
  28.3 1.4 copy-start.6
  36.7 4.8 copy-start.7
  58.8 4.0 copy-start.5
  58.8 53.6 %all-to-all-start.1 = ((bf16[256,8,512]{0,2,1:T(8,128)(2,1)}), bf16[256,8,512]{0,2,1:T(8,128)(2,1)S(1)}, u32[]{:S(2)}, u32[]{:S(2)}) async-start(bf16[256,8,512]{0,2,1:T(8,128)(2,1)} %bitcast.195), calls=%async_computation.1 | async-start | bytes 4194304 | tf_op jit(solution)/shard_map/all_to_all | solution.py:125
  112.4 1.3 copy-start.1
  112.4 6.5 %copy-start.8 = (f32[256]{0:T(256)S(1)}, f32[256]{0:T(256)}, u32[]{:S(2)}) copy-start(f32[256]{0:T(256)} %param.16) | copy-start | bytes 3076
  112.4 6.6 %copy-start.9 = (f32[256]{0:T(256)S(1)}, f32[256]{0:T(256)}, u32[]{:S(2)}) copy-start(f32[256]{0:T(256)} %param.17) | copy-start | bytes 3076
  113.7 188.4 %all-to-all-start.2 = ((bf16[256,8,2048]{0,2,1:T(8,128)(2,1)}), bf16[256,8,2048]{0,2,1:T(8,128)(2,1)}, u32[]{:S(2)}, u32[]{:S(2)}) async-start(bf16[256,8,2048]{0,2,1:T(8,128)(2,1)} %bitcast.191), calls=%async_computation.2 | async-start | bytes 16777216 | tf_op jit(solution)/shard_map/all_to_all | solution.py:118
  496.9 13.2 %collective-permute-start.2 = (f32[256,2048]{1,0:T(8,128)S(1)}, f32[256,2048]{1,0:T(8,128)}, u32[]{:S(2)}, u32[]{:S(2)}) collective-permute-start(f32[256,2048]{1,0:T(8,128)S(1)} %get-tuple-element.49), channel_id=1, source_target_pairs={{0,8},{8,16},{16,24},{1,9},{9,17},{17,25},{2,10},{10,18},{18,26},{... | collective-permute-start | bytes 6291464 | tf_op jit(solution)/shard_map/ppermute | solution.py:18
  509.0 18.4 %copy-start.10 = (f32[256]{0:T(256)S(1)}, f32[256]{0:T(256)}, u32[]{:S(2)}) copy-start(f32[256]{0:T(256)} %param.18) | copy-start | bytes 3076
  513.4 39.8 %collective-permute-start.3 = (f32[256,2048]{1,0:T(8,128)}, f32[256,2048]{1,0:T(8,128)}, u32[]{:S(2)}, u32[]{:S(2)}) collective-permute-start(f32[256,2048]{1,0:T(8,128)} %multiply_add_fusion.1), channel_id=1, source_target_pairs={{0,8},{8,16},{16,24},{1,9},{9,17},{17,25},{2,10},{10,18},{18,26},{... | collective-permute-start | bytes 6291464 | tf_op jit(solution)/shard_map/ppermute | solution.py:18
  556.1 30.4 %collective-permute-start.4 = (bf16[256,2048]{1,0:T(8,128)(2,1)}, bf16[256,2048]{1,0:T(8,128)(2,1)S(1)}, u32[]{:S(2)}, u32[]{:S(2)}) collective-permute-start(bf16[256,2048]{1,0:T(8,128)(2,1)} %multiply_add_fusion), channel_id=1, source_target_pairs={{0,8},{8,16},{16,24},{1,9},{9,17},{17,25},{2,10},{10,18},{18,26},{... | collective-permute-start | bytes 3145736 | tf_op jit(solution)/shard_map/ppermute | solution.py:18
  569.9 16.6 %copy-start = (bf16[8,256,1,512]{3,1,0,2:T(8,128)(2,1)S(1)}, bf16[8,256,1,512]{3,1,0,2:T(8,128)(2,1)}, u32[]{:S(2)}) copy-start(bf16[8,256,1,512]{3,1,0,2:T(8,128)(2,1)} %copy.95) | copy-start | bytes 6291460
where the time goes:
time: 611 us; the launch traced here: 607 us
  waiting for transfers between devices  186 us (30%)
  local copies, waits for them, and re-layouts  163 us (27%)
  matrix products  113 us (18%)
  other arithmetic  99.8 us (16%)
  starting transfers between devices  44.3 us (7%)
    all_to_all x1, waiting for transfers between devices, shards(): lax.all_to_all(x_ready.reshape(tok_dev, n_inner, ch_dev), 'inner', split_...  175 us
    reshape x9, local copies, waits for them, and re-layouts, head_columns(): jnp.broadcast_to(per_head[:, :, None], (rows, head_count, HEADDIM))  40.8 us
    convert_element_type x2, other arithmetic, causal_conv(): return jax.nn.silu(summed).astype(jnp.bfloat16)  34.1 us
    dot_general x8, matrix products, span_step(): jnp.einsum('hts,shp->thp', mixing, x_heads, preferred_element_type=jnp.fl...  33.6 us
    dot_general x8, matrix products, span_step(): jnp.dot(c_span, state.astype(jnp.bfloat16), preferred_element_type=jnp.fl...  32.4 us
    ppermute x5, starting transfers between devices, from_behind(): return lax.ppermute(x, axis, pairs)  27.8 us
    reshape x8, local copies, waits for them, and re-layouts, span_step(): y_intra = jnp.einsum('hts,shp->thp', mixing, x_heads, preferred_element_t...  23.5 us
    broadcast_in_dim x27, local copies, waits for them, and re-layouts, head_columns(): jnp.broadcast_to(per_head[:, :, None], (rows, head_count, HEADDIM))  21 us
  transfers between devices with their start and end apart: 8, of which 2 were waited for; matrix products, arithmetic and copies ran while one was open for 25% of the time, Pallas kernels for 0%

commit v1 on v0

--- a/solution.py
+++ b/solution.py
@@ -10,6 +10,22 @@
 GROUPS = 8
 CONV = 4
 SPAN = 256
+
+
+def pairwise_exchange(shard, axis, split, join):
+    ways, here = (lax.axis_size(axis), lax.axis_index(axis))
+    width = shard.shape[split] // ways
+    shape = list(shard.shape)
+    shape[split] = width
+    height = shape[join]
+    shape[join] = height * ways
+    full = jnp.zeros(shape, shard.dtype)
+    for mask in range(ways):
+        part = lax.dynamic_slice_in_dim(shard, (here ^ mask) * width, width, axis=split)
+        if mask:
+            part = lax.ppermute(part, axis, [(d, d ^ mask) for d in range(ways)])
+        full = lax.dynamic_update_slice_in_dim(full, part, (here ^ mask) * height, axis=join)
+    return full
 
 
 def from_behind(x, axis, by):
@@ -115,13 +131,7 @@
     bc_ready = causal_conv(bc_in, bc_prev, conv_bc_weight, conv_bc_bias)
     bc_send = group_copies(bc_ready, dest_group, n_inner)
     x_recv, bc_recv, dt_recv = (
-        lax.all_to_all(
-            x_ready.reshape(tok_dev, n_inner, ch_dev),
-            "inner",
-            split_axis=1,
-            concat_axis=0,
-            tiled=True,
-        ),
+        pairwise_exchange(x_ready.reshape(tok_dev, n_inner, ch_dev), "inner", 1, 0),
         lax.all_to_all(bc_send, "inner", split_axis=1, concat_axis=0, tiled=True),
         lax.all_to_all(dt_send, "inner", split_axis=1, concat_axis=0, tiled=True),
     )

time: 611 us -> 652 us (1.067)
  the two profiles are of different devices: /device:TPU:0 before, /device:TPU:17 now
where the time goes in v1:
time: 652 us; the launch traced here: 648 us
  local copies, waits for them, and re-layouts  210 us (32%)
  waiting for transfers between devices  188 us (29%)
  matrix products  112 us (17%)
  other arithmetic  101 us (15%)
  starting transfers between devices  36.3 us (6%)
    ppermute x7, waiting for transfers between devices, pairwise_exchange(): part = lax.ppermute(part, axis, [(d, d ^ mask) for d in range(ways)])  154 us
    convert_element_type x2, other arithmetic, causal_conv(): return jax.nn.silu(summed).astype(jnp.bfloat16)  44.9 us
    reshape x9, local copies, waits for them, and re-layouts, head_columns(): jnp.broadcast_to(per_head[:, :, None], (rows, head_count, HEADDIM))  41 us
    ppermute x5, waiting for transfers between devices, from_behind(): return lax.ppermute(x, axis, pairs)  34.2 us
    dot_general x8, matrix products, span_step(): jnp.einsum('hts,shp->thp', mixing, x_heads, preferred_element_type=jnp.fl...  33.4 us
    unnamed x38, local copies, waits for them, and re-layouts  32.7 us
    dot_general x8, matrix products, span_step(): jnp.dot(c_span, state.astype(jnp.bfloat16), preferred_element_type=jnp.fl...  32.4 us
    dynamic_slice x16, local copies, waits for them, and re-layouts, slab_core(): end_state, outputs = lax.scan(span_step, zero_state, inputs)  30.4 us
  transfers between devices with their start and end apart: 14, of which 7 were waited for; matrix products, arithmetic and copies ran while one was open for 27% of the time, Pallas kernels for 0%

profile of v1, /device:TPU:17, one launch (start us, length us, event | category | flops | bytes accessed | tf_op | source)
XLA Modules:
  0.0 648.0 jit_solution(498487599189432252)
XLA Ops:
  6.5 5.8 all-to-all-start
  20.6 11.9 %copy.132 = bf16[256,16384]{0,1:T(8,128)(2,1)} copy(bf16[256,16384]{1,0:T(8,128)(2,1)} %param.13) | data formatting | bytes 16777216 | tf_op args[0]
  38.5 7.0 %multiply_convert_fusion.4 = bf16[256,4096]{0,1:T(8,128)(2,1)S(1)} fusion(f32[259,4096]{0,1:T(8,128)S(1)} %maximum_convert_fusion.1, f32[4096]{0:T(1024)S(1)} %bitcast.202, f32[4096]{0:T(1024)S(1)} %bitcast.203, f32[4096]{0:T(1024)S(1)} %bitcast.201, f32[4096]{0:T(1024)S(1)} %bitcast.200, f32[4096]{0:T(1024)S(1)} %copy-done.7), kind=kLoop, calls=%fused_computation.65 | loop fusion | flops 13631488 | bytes 18956288 | tf_op jit(solution)/shard_map/convert_element_type | solution.py:44
  55.9 4.1 copy.131
  60.0 14.8 %maximum_convert_fusion = f32[259,16384]{0,1:T(8,128)} fusion(bf16[256,16384]{0,1:T(8,128)(2,1)} %copy.132, bf16[3,16384]{0,1:T(8,128)(2,1)} %copy.131), kind=kLoop, calls=%fused_computation.56 | loop fusion | flops 16973824 | bytes 25460736 | tf_op jit(solution)/shard_map/convert_element_type | solution.py:40
  74.8 5.2 all-to-all-start.1
  80.0 37.9 %multiply_convert_fusion.3 = bf16[256,16384]{0,1:T(8,128)(2,1)} fusion(f32[259,16384]{0,1:T(8,128)} %maximum_convert_fusion, f32[16384]{0:T(1024)S(1)} %bitcast.196, f32[16384]{0:T(1024)S(1)} %bitcast.197, f32[16384]{0:T(1024)S(1)} %bitcast.195, f32[16384]{0:T(1024)S(1)} %bitcast.194, f32[16384]{0:T(1024)S(1)} %copy-done.6), kind=kLoop, calls=%fused_computation.55 | loop fusion | flops 54525952 | bytes 75825152 | tf_op jit(solution)/shard_map/convert_element_type | solution.py:44
  117.9 5.8 constant_dynamic-slice_fusion.1
  141.8 4.5 broadcast_in_dim.88
  154.7 33.3 %collective-permute-done.3 = bf16[256,1,2048]{2,0,1:T(8,128)(2,1)} collective-permute-done((bf16[256,1,2048]{2,0,1:T(8,128)(2,1)}, bf16[256,1,2048]{2,0,1:T(8,128)(2,1)}, u32[]{:S(2)}, u32[]{:S(2)}) %collective-permute-start.3) | collective-permute-done | bytes 1048608 | tf_op jit(solution)/shard_map/ppermute | solution.py:26
  190.3 20.1 %collective-permute-done.4 = bf16[256,1,2048]{2,0,1:T(8,128)(2,1)} collective-permute-done((bf16[256,1,2048]{2,0,1:T(8,128)(2,1)}, bf16[256,1,2048]{2,0,1:T(8,128)(2,1)}, u32[]{:S(2)}, u32[]{:S(2)}) %collective-permute-start.4) | collective-permute-done | bytes 1048608 | tf_op jit(solution)/shard_map/ppermute | solution.py:26
  215.0 54.8 %collective-permute-done.6 = bf16[256,1,2048]{2,0,1:T(8,128)(2,1)} collective-permute-done((bf16[256,1,2048]{2,0,1:T(8,128)(2,1)}, bf16[256,1,2048]{2,0,1:T(8,128)(2,1)}, u32[]{:S(2)}, u32[]{:S(2)}) %collective-permute-start.6) | collective-permute-done | bytes 1048608 | tf_op jit(solution)/shard_map/ppermute | solution.py:26
  272.1 23.2 %collective-permute-done.7 = bf16[256,1,2048]{2,0,1:T(8,128)(2,1)S(1)} collective-permute-done((bf16[256,1,2048]{2,0,1:T(8,128)(2,1)}, bf16[256,1,2048]{2,0,1:T(8,128)(2,1)S(1)}, u32[]{:S(2)}, u32[]{:S(2)}) %collective-permute-start.7) | collective-permute-done | bytes 1048608 | tf_op jit(solution)/shard_map/ppermute | solution.py:26
  296.3 22.3 %collective-permute-done.8 = bf16[256,1,2048]{2,0,1:T(8,128)(2,1)S(1)} collective-permute-done((bf16[256,1,2048]{2,0,1:T(8,128)(2,1)}, bf16[256,1,2048]{2,0,1:T(8,128)(2,1)S(1)}, u32[]{:S(2)}, u32[]{:S(2)}) %collective-permute-start.8) | collective-permute-done | bytes 1048608 | tf_op jit(solution)/shard_map/ppermute | solution.py:26
  326.6 214.7 %while.13 = (s32[]{:T(128)}, f32[256,2048]{1,0:T(8,128)S(1)}, f32[8,256,2048]{2,1,0:T(8,128)}, f32[8,256,32]{1,2,0:T(8,128)}, bf16[8,256,256]{2,1,0:T(8,128)(2,1...) while((s32[]{:T(128)}, f32[256,2048]{1,0:T(8,128)S(1)}, ...), condition=%wide.region_3.4_spmd.clone, body=%wide.region_0.3_spmd.clone.sunk | while | flops 857301120 | bytes 35264520 | solution.py:94
  334.3 4.2 fusion.75
  361.2 4.2 fusion.75
  388.0 4.2 fusion.75
  414.9 4.2 fusion.75
  441.7 4.2 fusion.75
  453.2 4.1 fusion.76
  468.6 4.2 fusion.75
  495.4 4.2 fusion.75
  522.3 4.2 fusion.75
  546.4 9.1 %reduce-window.16 = f32[32,16,128]{2,1,0:T(8,128)S(1)} reduce-window(f32[32,16,128]{2,1,0:T(8,128)S(1)} %bitcast.191, f32[]{:T(128)} %constant.34.clone.1), window={size=1x1x128 pad=0_0x0_0x127_0}, to_apply=%region_4.5 | reduce-window | flops 8323072 | bytes 524292 | tf_op jit(solution)/shard_map/reduce-window.2
  556.6 11.5 %collective-permute-done.9 = f32[256,2048]{1,0:T(8,128)} collective-permute-done((f32[256,2048]{1,0:T(8,128)S(1)}, f32[256,2048]{1,0:T(8,128)}, u32[]{:S(2)}, u32[]{:S(2)}) %collective-permute-start.9) | collective-permute-done | bytes 2097184 | tf_op jit(solution)/shard_map/ppermute | solution.py:34
  570.1 4.7 collective-permute-start.10
  574.8 22.7 %collective-permute-done.10 = f32[256,2048]{1,0:T(8,128)S(1)} collective-permute-done((f32[256,2048]{1,0:T(8,128)S(1)}, f32[256,2048]{1,0:T(8,128)S(1)}, u32[]{:S(2)}, u32[]{:S(2)}) %collective-permute-start.10) | collective-permute-done | bytes 2097184 | tf_op jit(solution)/shard_map/ppermute | solution.py:34
  598.9 4.4 collective-permute-start.11
  603.6 7.9 %broadcast_in_dim.92 = f32[2048,32,64]{0,2,1:T(8,128)} broadcast(f32[2048,32]{0,1:T(8,128)S(1)} %fusion.50), dimensions={0,1} | broadcast | bytes 17039360 | tf_op jit(solution)/shard_map/broadcast_in_dim | solution.py:49
  611.5 17.8 %copy.145 = f32[2048,2048]{1,0:T(8,128)} copy(f32[2048,2048]{0,1:T(8,128)} %bitcast.181) | data formatting | bytes 33554432 | tf_op jit(solution)/shard_map/reshape | solution.py:49
  629.3 18.7 %fusion.31 = bf16[2048,2048]{1,0:T(8,128)(2,1)} fusion(f32[8,256,2048]{2,1,0:T(8,128)} %get-tuple-element.48, f32[2048,2048]{1,0:T(8,128)} %copy.145, bf16[2048,1,2048]{2,0,1:T(8,128)(2,1)} %constant_dynamic-update-slice_fusion, f32[2048]{0:T(1024)S(1)} %mul.240, bf16[256,2048]{1,0:T(8,128)(2,1)} %collective-permute-done.11, bf16[2048,512]{1,0:T(8,128)(2,1)S(1)} %bitcast.185), kind=kOutput, calls=%fused_computation.53 | convolution fusion | flops 2172649472 | bytes 52436992 | tf_op jit(solution)/shard_map/dot_general | solution.py:156
  (264 shorter events, 262.2 us)
Async XLA Ops:
  1.7 54.2 %collective-permute-start.1 = (bf16[3,16384]{1,0:T(4,128)(2,1)}, bf16[3,16384]{1,0:T(4,128)(2,1)}, u32[]{:S(2)}, u32[]{:S(2)}) collective-permute-start(bf16[3,16384]{1,0:T(4,128)(2,1)} %slice.90), channel_id=1, source_target_pairs={{0,1},{1,2},{2,3},{3,4},{4,5},{5,6},{6,7},{7,8},{8,9},{9,10},{10,1... | collective-permute-start | bytes 294920 | tf_op jit(solution)/shard_map/ppermute | solution.py:34
  6.5 68.4 %all-to-all-start = ((bf16[256,8,32]{0,2,1:T(8,128)(2,1)}), bf16[256,8,32]{0,2,1:T(8,128)(2,1)S(1)}, u32[]{:S(2)}, u32[]{:S(2)}) async-start(bf16[256,8,32]{0,2,1:T(8,128)(2,1)} %bitcast), calls=%async_computation | async-start | bytes 262144 | tf_op jit(solution)/shard_map/all_to_all | solution.py:136
  13.1 22.8 %collective-permute-start = (bf16[3,4096]{1,0:T(4,128)(2,1)S(1)}, bf16[3,4096]{1,0:T(4,128)(2,1)}, u32[]{:S(2)}, u32[]{:S(2)}) collective-permute-start(bf16[3,4096]{1,0:T(4,128)(2,1)S(1)} %slice.80), channel_id=1, source_target_pairs={{0,1},{1,2},{2,3},{3,4},{4,5},{5,6},{6,7},{7,8},{8,9},{9,10},{10,1... | collective-permute-start | bytes 73736 | tf_op jit(solution)/shard_map/ppermute | solution.py:34
  37.1 1.4 copy-start.3
  37.2 1.4 copy-start.4
  37.2 1.4 copy-start.5
  37.2 1.4 copy-start.7
  45.5 4.8 copy-start.8
  60.0 20.0 %copy-start.6 = (f32[16384]{0:T(1024)S(1)}, f32[16384]{0:T(1024)}, u32[]{:S(2)}) copy-start(f32[16384]{0:T(1024)} %param.20) | copy-start | bytes 196612
  74.8 76.2 %copy-start.2 = (bf16[256,8,32]{0,2,1:T(8,128)(2,1)}, bf16[256,8,32]{0,2,1:T(8,128)(2,1)S(1)}, u32[]{:S(2)}) copy-start(bf16[256,8,32]{0,2,1:T(8,128)(2,1)S(1)} %all-to-all-done) | copy-start | bytes 393220
  74.8 244.8 %all-to-all-start.1 = ((bf16[256,8,512]{0,2,1:T(8,128)(2,1)}), bf16[256,8,512]{0,2,1:T(8,128)(2,1)}, u32[]{:S(2)}, u32[]{:S(2)}) async-start(bf16[256,8,512]{0,2,1:T(8,128)(2,1)} %bitcast.10), calls=%async_computation.1 | async-start | bytes 4194304 | tf_op jit(solution)/shard_map/all_to_all | solution.py:135
  123.7 7.8 %copy-start.9 = (f32[256]{0:T(256)S(1)}, f32[256]{0:T(256)}, u32[]{:S(2)}) copy-start(f32[256]{0:T(256)} %param.17) | copy-start | bytes 3076
  123.7 7.9 %copy-start.10 = (f32[256]{0:T(256)S(1)}, f32[256]{0:T(256)}, u32[]{:S(2)}) copy-start(f32[256]{0:T(256)} %param.16) | copy-start | bytes 3076
  126.0 26.0 %collective-permute-start.2 = (bf16[256,1,2048]{2,0,1:T(8,128)(2,1)}, bf16[256,1,2048]{2,0,1:T(8,128)(2,1)}, u32[]{:S(2)}, u32[]{:S(2)}) collective-permute-start(bf16[256,1,2048]{2,0,1:T(8,128)(2,1)} %copy.149), channel_id=1, source_target_pairs={{0,1},{1,0},{2,3},{3,2},{4,5},{5,4},{6,7},{7,6},{8,9},{9,8},{10,11... | collective-permute-start | bytes 3145736 | tf_op jit(solution)/shard_map/ppermute | solution.py:26
  128.6 59.3 %collective-permute-start.3 = (bf16[256,1,2048]{2,0,1:T(8,128)(2,1)}, bf16[256,1,2048]{2,0,1:T(8,128)(2,1)}, u32[]{:S(2)}, u32[]{:S(2)}) collective-permute-start(bf16[256,1,2048]{2,0,1:T(8,128)(2,1)} %copy.150), channel_id=1, source_target_pairs={{0,2},{1,3},{2,0},{3,1},{4,6},{5,7},{6,4},{7,5},{8,10},{9,11},{10,... | collective-permute-start | bytes 3145736 | tf_op jit(solution)/shard_map/ppermute | solution.py:26
  131.3 79.2 %collective-permute-start.4 = (bf16[256,1,2048]{2,0,1:T(8,128)(2,1)}, bf16[256,1,2048]{2,0,1:T(8,128)(2,1)}, u32[]{:S(2)}, u32[]{:S(2)}) collective-permute-start(bf16[256,1,2048]{2,0,1:T(8,128)(2,1)} %copy.151), channel_id=1, source_target_pairs={{0,3},{1,2},{2,1},{3,0},{4,7},{5,6},{6,5},{7,4},{8,11},{9,10},{10,... | collective-permute-start | bytes 3145736 | tf_op jit(solution)/shard_map/ppermute | solution.py:26
  136.3 76.5 %collective-permute-start.5 = (bf16[256,1,2048]{2,0,1:T(8,128)(2,1)}, bf16[256,1,2048]{2,0,1:T(8,128)(2,1)}, u32[]{:S(2)}, u32[]{:S(2)}) collective-permute-start(bf16[256,1,2048]{2,0,1:T(8,128)(2,1)} %copy.152), channel_id=1, source_target_pairs={{0,4},{1,5},{2,6},{3,7},{4,0},{5,1},{6,2},{7,3},{8,12},{9,13},{10,... | collective-permute-start | bytes 3145736 | tf_op jit(solution)/shard_map/ppermute | solution.py:26
  138.6 7.7 %copy-start.1 = (bf16[256,1,2048]{2,0,1:T(8,128)(2,1)S(1)}, bf16[256,1,2048]{2,0,1:T(8,128)(2,1)}, u32[]{:S(2)}) copy-start(bf16[256,1,2048]{2,0,1:T(8,128)(2,1)} %copy.148) | copy-start | bytes 3145732
  138.6 131.3 %collective-permute-start.6 = (bf16[256,1,2048]{2,0,1:T(8,128)(2,1)}, bf16[256,1,2048]{2,0,1:T(8,128)(2,1)}, u32[]{:S(2)}, u32[]{:S(2)}) collective-permute-start(bf16[256,1,2048]{2,0,1:T(8,128)(2,1)} %copy.153), channel_id=1, source_target_pairs={{0,5},{1,4},{2,7},{3,6},{4,1},{5,0},{6,3},{7,2},{8,13},{9,12},{10,... | collective-permute-start | bytes 3145736 | tf_op jit(solution)/shard_map/ppermute | solution.py:26
  152.1 143.2 %collective-permute-start.7 = (bf16[256,1,2048]{2,0,1:T(8,128)(2,1)}, bf16[256,1,2048]{2,0,1:T(8,128)(2,1)S(1)}, u32[]{:S(2)}, u32[]{:S(2)}) collective-permute-start(bf16[256,1,2048]{2,0,1:T(8,128)(2,1)} %copy.154), channel_id=1, source_target_pairs={{0,6},{1,7},{2,4},{3,5},{4,2},{5,3},{6,0},{7,1},{8,14},{9,15},{10,... | collective-permute-start | bytes 3145736 | tf_op jit(solution)/shard_map/ppermute | solution.py:26
  188.0 130.7 %collective-permute-start.8 = (bf16[256,1,2048]{2,0,1:T(8,128)(2,1)}, bf16[256,1,2048]{2,0,1:T(8,128)(2,1)S(1)}, u32[]{:S(2)}, u32[]{:S(2)}) collective-permute-start(bf16[256,1,2048]{2,0,1:T(8,128)(2,1)} %copy.155), channel_id=1, source_target_pairs={{0,7},{1,6},{2,5},{3,4},{4,3},{5,2},{6,1},{7,0},{8,15},{9,14},{10,... | collective-permute-start | bytes 3145736 | tf_op jit(solution)/shard_map/ppermute | solution.py:26
  541.4 26.8 %collective-permute-start.9 = (f32[256,2048]{1,0:T(8,128)S(1)}, f32[256,2048]{1,0:T(8,128)}, u32[]{:S(2)}, u32[]{:S(2)}) collective-permute-start(f32[256,2048]{1,0:T(8,128)S(1)} %get-tuple-element.49), channel_id=1, source_target_pairs={{0,8},{8,16},{16,24},{1,9},{9,17},{17,25},{2,10},{10,18},{18,26},{... | collective-permute-start | bytes 6291464 | tf_op jit(solution)/shard_map/ppermute | solution.py:34
  556.1 47.2 %copy-start.11 = (f32[256]{0:T(256)S(1)}, f32[256]{0:T(256)}, u32[]{:S(2)}) copy-start(f32[256]{0:T(256)} %param.18) | copy-start | bytes 3076
  570.1 27.5 %collective-permute-start.10 = (f32[256,2048]{1,0:T(8,128)S(1)}, f32[256,2048]{1,0:T(8,128)S(1)}, u32[]{:S(2)}, u32[]{:S(2)}) collective-permute-start(f32[256,2048]{1,0:T(8,128)S(1)} %multiply_add_fusion.1), channel_id=1, source_target_pairs={{0,8},{8,16},{16,24},{1,9},{9,17},{17,25},{2,10},{10,18},{18,26},{... | collective-permute-start | bytes 6291464 | tf_op jit(solution)/shard_map/ppermute | solution.py:34
  598.9 30.4 %collective-permute-start.11 = (bf16[256,2048]{1,0:T(8,128)(2,1)}, bf16[256,2048]{1,0:T(8,128)(2,1)}, u32[]{:S(2)}, u32[]{:S(2)}) collective-permute-start(bf16[256,2048]{1,0:T(8,128)(2,1)} %multiply_add_fusion), channel_id=1, source_target_pairs={{0,8},{8,16},{16,24},{1,9},{9,17},{17,25},{2,10},{10,18},{18,26},{... | collective-permute-start | bytes 3145736 | tf_op jit(solution)/shard_map/ppermute | solution.py:34
  611.5 17.8 %copy-start = (bf16[8,256,1,512]{3,1,0,2:T(8,128)(2,1)S(1)}, bf16[8,256,1,512]{3,1,0,2:T(8,128)(2,1)}, u32[]{:S(2)}) copy-start(bf16[8,256,1,512]{3,1,0,2:T(8,128)(2,1)} %copy.130) | copy-start | bytes 6291460
